TPU v7x, 32 devices: a whole 2x2x4 slice. The times are simulated.
32 devices in a mesh: parts: 2 (over y), ctx: 4 (over z), opt: 4 (over x, core).
Axes of the slice: x: 2, y: 2, z: 4, core: 2. Of those that a mesh axis runs over, the one named last changes fastest.
Arguments:
- options: bfloat16 [8, 32, 3072], P(('parts', 'opt'), 'ctx'), parts along dimension 0, may hold values from -6 to 6
- cache_keys: bfloat16 [1024, 512], P(('parts', 'ctx')), parts along dimension 0, may hold values from -800 to 800
- cache_values: bfloat16 [1024, 512], P(('parts', 'ctx')), parts along dimension 0, may hold values from -6 to 6
- attention_gain: float32 [3072], replicated, may hold values from 0.5 to 1.5
- expert_gain: float32 [3072], replicated, may hold values from 0.5 to 1.5
- input_weight: bfloat16 [3072, 4096], P(None, 'ctx'), may hold values from -0.109375 to 0.109375
- output_weight: bfloat16 [3072, 3072], P(None, 'ctx'), may hold values from -0.875 to 0.875
- router_weight: bfloat16 [3072, 8], replicated, may hold values from -0.109375 to 0.109375
- gate_weight: bfloat16 [3072, 65536], P(None, ('ctx', 'opt')), may hold values from -0.109375 to 0.109375
- up_weight: bfloat16 [3072, 65536], P(None, ('ctx', 'opt')), may hold values from -0.109375 to 0.109375
- down_weight: bfloat16 [65536, 3072], P(('ctx', 'opt')), may hold values from -0.0625 to 0.0625
- routing: int32 [8, 32, 2], P(('parts', 'opt'), 'ctx'), parts along dimension 0, may hold values from 0 to 7, all different within a row; in each aligned block of 8 rows (0 to 7, 8 to 15, ..., all dimensions but the last counted through in order) at most 4 rows name the same one
Outputs:
- layer_out: bfloat16 [8, 32, 3072], P(('parts', 'opt'), 'ctx'), parts along dimension 0
There are 2 independent parts, one for each index of `parts`. A program takes and returns all parts, laid end to end along the dimension named above; an argument that names none is the same for every part. Nothing has to cross between parts.
Inputs may be any that keep to these rules, and one draw needn't show every extreme that they name: `routing`: at most 4 of the 8 rows of one device name the same expert, and in some device one expert is named by exactly 4 rows; the two experts of a row differ.
All inputs are finite; a program needn't handle non-finite values.
Results may differ from a plain program's by a relative error of at most 0.018.
Values may be sent and summed in bfloat16 or wider, within the bound.
No kernel may reach another device: no remote copies, remote signals or barrier semaphores. Data moves between devices by JAX's collectives and lax.ppermute only.
A program may use at most 192 MiB of HBM per device.

v0:
```python
import jax
import jax.numpy as jnp
from jax import lax
from jax.sharding import PartitionSpec as P

H = 24
KVH = 4
HD = 128
FF = 8192
MOST = 4


EPS = 1e-05
THETA = 1000000.0


def combined_all(x, axis, combine):
    everything = jax.tree.map(
        lambda part, kind: lax.all_gather(part.astype(kind), axis),
        x,
        (jnp.bfloat16, jnp.bfloat16, jnp.bfloat16),
    )

    def take(k):
        return jax.tree.map(lambda part, own: part[k].astype(own.dtype), everything, x)

    return lax.fori_loop(
        1, lax.axis_size(axis), lambda k, so_far: combine(so_far, take(k)), take(0)
    )


def rms_scale(row_data, gain_vector):
    floats = row_data.astype(jnp.float32)
    factor = lax.rsqrt(jnp.mean(floats * floats, axis=-1, keepdims=True) + EPS)
    return (floats * factor * gain_vector).astype(jnp.bfloat16)


def rotate(tile_data, first_head, positions):
    row_count, tile_width = tile_data.shape
    head_count = tile_width // HD
    half_dim = HD // 2
    split_view = tile_data.reshape(row_count, head_count, 2, half_dim)
    inverse = THETA ** (-2.0 * jnp.arange(half_dim, dtype=jnp.float32) / HD)
    angles = positions.astype(jnp.float32)[:, None] * inverse[None, :]
    cosine = jnp.cos(angles)[:, None, :]
    sine_part = jnp.sin(angles)[:, None, :]
    lower_half = split_view[:, :, 0]
    upper_half = split_view[:, :, 1]
    turned = jnp.stack(
        [
            lower_half * cosine - upper_half * sine_part,
            upper_half * cosine + lower_half * sine_part,
        ],
        axis=2,
    )
    rotated_head = first_head + jnp.arange(head_count) < H + KVH
    return jnp.where(rotated_head[None, :, None, None], turned, split_view).reshape(
        row_count, tile_width
    )


def softmax_parts(queries, key_rows, value_rows, key_start, cached):
    key_count = key_rows.shape[0]
    key_heads = key_rows.reshape(key_count, KVH, HD)
    value_heads = value_rows.reshape(key_count, KVH, HD).astype(jnp.float32)
    scores = jnp.einsum(
        "rhgd,khd->hgrk", queries, key_heads, preferred_element_type=jnp.float32
    ) * HD ** (-0.5)
    query_index = jnp.arange(queries.shape[0])
    key_index = jnp.arange(key_count)
    visible = (key_index[None, :] < cached) | (
        key_start + key_index[None, :] - cached <= query_index[:, None]
    )
    scores = jnp.where(visible, scores, -jnp.inf)
    maxima = jnp.max(scores, axis=-1)
    weights = jnp.exp(scores - maxima[..., None])
    totals = jnp.sum(weights, axis=-1)
    summed = jnp.einsum("hgrk,khd->hgrd", weights, value_heads, precision=lax.Precision.HIGHEST)
    return (maxima, totals, summed)


def join_parts(first, second):
    first_max, first_total, first_sum = first
    second_max, second_total, second_sum = second
    larger = jnp.maximum(first_max, second_max)
    first_scale = jnp.exp(first_max - larger)
    second_scale = jnp.exp(second_max - larger)
    return (
        larger,
        first_total * first_scale + second_total * second_scale,
        first_sum * first_scale[..., None] + second_sum * second_scale[..., None],
    )


def shards(
    options,
    cache_keys,
    cache_values,
    attention_gain,
    expert_gain,
    input_weight,
    output_weight,
    router_weight,
    gate_weight,
    up_weight,
    down_weight,
    routing,
):
    own_rows = options[0]
    ctx_count = lax.axis_size("ctx")
    ctx_here = lax.axis_index("ctx")
    local_rows = own_rows.shape[0]
    passage = cache_keys.shape[0] * ctx_count
    tile_columns = input_weight.shape[1]
    first_head = ctx_here * (tile_columns // HD)
    normed = rms_scale(own_rows, attention_gain)
    row_piece = lax.all_gather(normed, "ctx", axis=0, tiled=True)
    product = jnp.dot(row_piece, input_weight, preferred_element_type=jnp.float32)
    where_at = passage + jnp.int32(0) + jnp.arange(row_piece.shape[0])
    rotated_tile = rotate(product, first_head, where_at).astype(jnp.bfloat16)
    projected = lax.all_gather(rotated_tile, "ctx", axis=1, tiled=True)
    option_len = projected.shape[0]
    query_width = H * HD
    key_end = (H + KVH) * HD
    queries = projected[:, :query_width].reshape(option_len, KVH, H // KVH, HD)
    option_keys = projected[:, query_width:key_end]
    option_values = projected[:, key_end:]
    own_start = ctx_here * local_rows
    own_keys = lax.dynamic_slice_in_dim(option_keys, own_start, local_rows, 0)
    own_values = lax.dynamic_slice_in_dim(option_values, own_start, local_rows, 0)
    key_rows = jnp.concatenate([cache_keys, own_keys], axis=0)
    value_rows = jnp.concatenate([cache_values, own_values], axis=0)
    local_max, local_total, local_sum = softmax_parts(
        queries, key_rows, value_rows, own_start, cache_keys.shape[0]
    )
    maxima, totals, summed = combined_all((local_max, local_total, local_sum), "ctx", join_parts)
    attention = (
        (summed / totals[..., None])
        .transpose(2, 0, 1, 3)
        .reshape(option_len, query_width)
        .astype(jnp.bfloat16)
    )
    columns = jnp.dot(attention, output_weight, preferred_element_type=jnp.float32).astype(
        jnp.bfloat16
    )
    attention_out = lax.all_to_all(columns, "ctx", split_axis=0, concat_axis=1, tiled=True)
    mixed_in = (own_rows.astype(jnp.float32) + attention_out.astype(jnp.float32)).astype(
        jnp.bfloat16
    )
    expert_in = rms_scale(mixed_in, expert_gain)
    chosen_ids = routing[0]
    top_count = chosen_ids.shape[1]
    expert_count = router_weight.shape[1]
    logits = jnp.dot(expert_in, router_weight, preferred_element_type=jnp.float32)
    matches = chosen_ids[:, :, None] == jnp.arange(expert_count)[None, None, :]
    picked = jnp.sum(jnp.where(matches, logits[:, None, :], 0.0), axis=-1)
    gate_share = jax.nn.softmax(picked, axis=-1)
    ctx_width = expert_count * FF // ctx_count
    first_target = chosen_ids * FF // ctx_width
    last_target = ((chosen_ids + 1) * FF - 1) // ctx_width
    destination = jnp.arange(ctx_count)
    goes_to = (destination[None, None, :] >= first_target[:, :, None]) & (
        destination[None, None, :] <= last_target[:, :, None]
    )
    flat_goes = goes_to.reshape(local_rows * top_count, ctx_count).astype(jnp.int32)
    slot_index = jnp.cumsum(flat_goes, axis=0) - flat_goes
    slot_count = MOST * max(1, expert_count // ctx_count)
    slot_match = (flat_goes[:, :, None] == 1) & (
        slot_index[:, :, None] == jnp.arange(slot_count)[None, None, :]
    )
    slot_match = slot_match.reshape(local_rows, top_count, ctx_count * slot_count)
    token_slots = jnp.any(slot_match, axis=1).astype(jnp.bfloat16)
    model_width = expert_in.shape[1]
    outgoing = jnp.einsum(
        "rs,rd->sd", token_slots, expert_in, preferred_element_type=jnp.float32
    ).astype(jnp.bfloat16)
    outgoing = outgoing.reshape(ctx_count, slot_count, model_width)
    outgoing_ids = jnp.sum(jnp.where(slot_match, chosen_ids[:, :, None] + 1, 0), axis=(0, 1)) - 1
    outgoing_ids = outgoing_ids.reshape(ctx_count, slot_count)
    arrived, arrived_ids = (
        lax.all_to_all(outgoing, "ctx", split_axis=0, concat_axis=0, tiled=True),
        lax.all_to_all(outgoing_ids, "ctx", split_axis=0, concat_axis=0, tiled=True),
    )
    pooled, pooled_ids = (
        lax.all_gather(arrived, "opt", axis=0, tiled=True),
        lax.all_gather(arrived_ids, "opt", axis=0, tiled=True),
    )
    pooled = pooled.reshape(-1, model_width)
    pooled_ids = pooled_ids.reshape(-1)
    local_width = gate_weight.shape[1]
    opt_count = lax.axis_size("opt")
    column_start = (ctx_here * opt_count + lax.axis_index("opt")) * local_width
    column_expert = (column_start + jnp.arange(local_width)) // FF
    owned_mask = pooled_ids[:, None] == column_expert[None, :]
    gate_part = jnp.dot(pooled, gate_weight, preferred_element_type=jnp.float32)
    up_part = jnp.dot(pooled, up_weight, preferred_element_type=jnp.float32)
    hidden = jnp.where(owned_mask, jax.nn.silu(gate_part) * up_part, 0.0).astype(jnp.bfloat16)
    partial_out = jnp.dot(hidden, down_weight, preferred_element_type=jnp.float32)
    summed_back = lax.psum_scatter(
        partial_out.astype(jnp.bfloat16), "opt", scatter_dimension=0, tiled=True
    ).astype(jnp.float32)
    returned = lax.all_to_all(
        summed_back.reshape(ctx_count, slot_count, model_width).astype(jnp.bfloat16),
        "ctx",
        split_axis=0,
        concat_axis=0,
        tiled=True,
    ).astype(jnp.float32)
    weighting = jnp.sum(jnp.where(slot_match, gate_share[:, :, None], 0.0), axis=1)
    expert_sum = jnp.dot(
        weighting,
        returned.reshape(-1, model_width),
        precision=lax.Precision.HIGHEST,
        preferred_element_type=jnp.float32,
    )
    layer_out = (mixed_in.astype(jnp.float32) + expert_sum).astype(jnp.bfloat16)
    return layer_out[None]


def solution(mesh):
    placed = (
        P(("parts", "opt"), "ctx", None),
        P(("parts", "ctx"), None),
        P(("parts", "ctx"), None),
        P(),
        P(),
        P(None, "ctx"),
        P(None, "ctx"),
        P(),
        P(None, ("ctx", "opt")),
        P(None, ("ctx", "opt")),
        P(("ctx", "opt"), None),
        P(("parts", "opt"), "ctx", None),
    )
    return jax.shard_map(
        shards,
        mesh=mesh,
        in_specs=placed,
        out_specs=P(("parts", "opt"), "ctx", None),
        check_vma=False,
    )
```

profile of v0, /device:TPU:0, one launch (start us, length us, event | category | flops | bytes accessed | tf_op | source)
XLA Modules:
  0.0 205.8 jit_solution(10806923455617362431)
XLA Ops:
  6.6 0.9 fusion.27
  7.5 0.1 broadcast_in_dim.97
  7.6 0.1 broadcast_in_dim.98
  7.7 0.9 fusion.29
  8.6 15.5 %all_gather.26 = bf16[32,3072]{1,0:T(8,128)(2,1)S(1)} all-gather(bf16[8,3072]{1,0:T(8,128)(2,1)S(1)} %fusion.29), channel_id=1, replica_groups=mesh['parts'=2,'ctx'=4,'opt'=4] {'ctx'}, dimensions={0}, use_global_device_ids=true | all-gather | bytes 245760 | tf_op jit(solution)/shard_map/all_gather | solution.py:117
  24.1 4.0 %fusion.52 = f32[32,1024]{1,0:T(8,128)S(1)} fusion(bf16[32,3072]{1,0:T(8,128)(2,1)S(1)} %all_gather.26, bf16[3072,1024]{1,0:T(8,128)(2,1)} %param.19), kind=kOutput, calls=%fused_computation.113 | convolution fusion | flops 201326592 | bytes 6619136 | tf_op jit(solution)/shard_map/dot_general | solution.py:118
  28.1 0.2 reshape.417
  28.3 0.1 multiply_cosine_fusion
  28.4 0.4 multiply_subtract_fusion
  28.8 0.4 pad_maximum_fusion
  29.2 0.1 stack.8
  29.3 14.3 %all_gather.27 = bf16[32,4096]{1,0:T(8,128)(2,1)S(1)} all-gather(bf16[32,1024]{1,0:T(8,128)(2,1)S(1)} %select_convert_fusion), channel_id=1, replica_groups=mesh['parts'=2,'ctx'=4,'opt'=4] {'ctx'}, dimensions={1}, use_global_device_ids=true | all-gather | bytes 327680 | tf_op jit(solution)/shard_map/all_gather | solution.py:121
  43.7 0.3 reshape.419
  44.1 0.4 fusion.51
  44.5 0.3 fusion.17
  44.9 0.6 convolution_convert_fusion.2
  45.5 13.2 %all-gather = bf16[16,6,32]{2,1,0:T(8,128)(2,1)S(1)} all-gather(bf16[4,6,32]{2,1,0:T(8,128)(2,1)S(1)} %convert_element_type.182), channel_id=2, replica_groups=mesh['parts'=2,'ctx'=4,'opt'=4] {'ctx'}, dimensions={0}, use_global_device_ids=true | all-gather | bytes 7680 | tf_op jit(solution)/shard_map/all_gather | solution.py:19
  58.6 13.2 %all-gather.1 = bf16[16,6,32]{2,1,0:T(8,128)(2,1)S(1)} all-gather(bf16[4,6,32]{2,1,0:T(8,128)(2,1)S(1)} %fusion.17), channel_id=3, replica_groups=mesh['parts'=2,'ctx'=4,'opt'=4] {'ctx'}, dimensions={0}, use_global_device_ids=true | all-gather | bytes 7680 | tf_op jit(solution)/shard_map/all_gather | solution.py:19
  71.8 15.6 %all-gather.2 = bf16[16,6,32,128]{3,2,1,0:T(8,128)(2,1)S(1)} all-gather(bf16[4,6,32,128]{3,2,1,0:T(8,128)(2,1)S(1)} %convolution_convert_fusion.2), channel_id=4, replica_groups=mesh['parts'=2,'ctx'=4,'opt'=4] {'ctx'}, dimensions={0}, use_global_device_ids=true | all-gather | bytes 983040 | tf_op jit(solution)/shard_map/all_gather | solution.py:19
  87.5 1.4 while.19
  87.6 0.4 fusion.66
  88.0 0.4 fusion.66
  88.5 0.4 fusion.66
  88.9 0.2 fusion.21
  89.1 0.1 copy.35
  89.2 0.2 convert_element_type.195
  89.4 3.8 %fusion.10 = bf16[4,8,768]{2,1,0:T(8,128)(2,1)} fusion(bf16[32,3072]{1,0:T(8,128)(2,1)S(1)} %convert_element_type.195, bf16[3072,768]{1,0:T(8,128)(2,1)} %param.20), kind=kOutput, calls=%fused_computation.22 | convolution fusion | flops 151019520 | bytes 4964352 | tf_op jit(solution)/shard_map/dot_general | solution.py:143
  93.2 5.0 %all-to-all-start = ((bf16[4,8,768]{2,1,0:T(8,128)(2,1)}), bf16[4,8,768]{2,1,0:T(8,128)(2,1)S(1)}, u32[]{:S(2)}, u32[]{:S(2)}) async-start(bf16[4,8,768]{2,1,0:T(8,128)(2,1)} %fusion.10), calls=%async_computation | async-start | bytes 98304 | tf_op jit(solution)/shard_map/all_to_all | solution.py:146
  98.3 0.1 eq.71
  98.4 0.1 copy.36
  98.5 0.1 mul.249
  98.5 0.1 copy.37
  98.6 0.1 add.203
  98.7 0.1 fusion.37
  98.8 0.1 fusion.41
  98.9 0.1 select_reduce_fusion
  99.0 0.1 and.72
  99.1 0.1 and.73
  99.2 0.1 eq.68
  99.3 0.1 eq.69
  99.4 0.6 broadcast_add_fusion
  100.0 4.1 %all-to-all-done = bf16[4,8,768]{2,1,0:T(8,128)(2,1)S(1)} async-done(((bf16[4,8,768]{2,1,0:T(8,128)(2,1)}), bf16[4,8,768]{2,1,0:T(8,128)(2,1)S(1)}, u32[]{:S(2)}, u32[]{:S(2)}) %all-to-all-start) | async-done | bytes 49184 | tf_op jit(solution)/shard_map/all_to_all | solution.py:146
  104.1 3.2 %all-to-all-start.1 = ((s32[4,1,8]{2,1,0:T(1,128)}), s32[4,1,8]{2,1,0:T(1,128)S(1)}, u32[]{:S(2)}, u32[]{:S(2)}) async-start(s32[4,1,8]{2,1,0:T(1,128)} %bitcast.18), calls=%async_computation.1 | async-start | bytes 4096 | tf_op jit(solution)/shard_map/all_to_all | solution.py:182
  107.3 0.1 fusion.24
  107.5 0.9 fusion.5
  108.4 4.3 %all-to-all-done.1 = s32[4,1,8]{2,1,0:T(1,128)S(1)} async-done(((s32[4,1,8]{2,1,0:T(1,128)}), s32[4,1,8]{2,1,0:T(1,128)S(1)}, u32[]{:S(2)}, u32[]{:S(2)}) %all-to-all-start.1) | async-done | bytes 160 | tf_op jit(solution)/shard_map/all_to_all | solution.py:182
  112.7 3.4 %all-to-all-start.2 = ((bf16[4,8,3072]{2,1,0:T(8,128)(2,1)}), bf16[4,8,3072]{2,1,0:T(8,128)(2,1)S(1)}, u32[]{:S(2)}, u32[]{:S(2)}) async-start(bf16[4,8,3072]{2,1,0:T(8,128)(2,1)} %fusion.5), calls=%async_computation.2 | async-start | bytes 393216 | tf_op jit(solution)/shard_map/all_to_all | solution.py:181
  116.1 0.0 reduce-scatter.2.cloned.1.call-start
  116.2 5.2 %all-gather.3 = s32[16,1,8]{2,1,0:T(1,128)S(1)} all-gather(s32[4,1,8]{2,1,0:T(1,128)S(1)} %all-to-all-done.1), channel_id=5, replica_groups=mesh['parts'=2,'ctx'=4,'opt'=4] {'opt'}, dimensions={0}, use_global_device_ids=true | all-gather | bytes 640 | tf_op jit(solution)/shard_map/all_gather | solution.py:186
  121.4 0.5 broadcast.422
  121.9 0.7 reduce.4
  122.5 0.1 eq.80
  122.6 8.9 %all_gather.33 = bf16[16,8,3072]{2,1,0:T(8,128)(2,1)S(1)} all-gather(bf16[4,8,3072]{2,1,0:T(8,128)(2,1)S(1)} %all-to-all-done.2), channel_id=1, replica_groups=mesh['parts'=2,'ctx'=4,'opt'=4] {'opt'}, dimensions={0}, use_global_device_ids=true | all-gather | bytes 983040 | tf_op jit(solution)/shard_map/all_gather | solution.py:185
  131.5 10.0 %fusion.15 = f32[128,4096]{1,0:T(8,128)S(1)} fusion(bf16[3072,4096]{1,0:T(8,128)(2,1)} %param.22, bf16[16,8,3072]{2,1,0:T(8,128)(2,1)S(1)} %all_gather.33), kind=kOutput, calls=%fused_computation.26 | convolution fusion | flops 3221225472 | bytes 28049408 | tf_op jit(solution)/shard_map/dot_general | solution.py:195
  141.5 20.0 %convolution_convert_fusion = bf16[128,3072]{1,0:T(8,128)(2,1)} fusion(bf16[4096,3072]{1,0:T(8,128)(2,1)} %param.24, bf16[3072,4096]{1,0:T(8,128)(2,1)} %param.23, f32[128,4096]{1,0:T(8,128)S(1)} %fusion.15, s32[4096]{0:T(1024)S(1)} %add_select_fusion, s32[128]{0:T(128)S(1)} %eq.80, bf16[16,8,3072]{2,1,0:T(8,128)(2,1)S(1)} %all_gather.33), kind=kOutput, calls=%fused_computation.11 | convolution fusion | flops 6447038464 | bytes 54018560 | tf_op jit(solution)/shard_map/dot_general | solution.py:198
  161.5 0.0 reduce-scatter.2.cloned.1.call-update
  161.5 0.2 fusion.39
  161.7 0.2 select_reduce_fusion.2
  161.9 24.3 %reduce-scatter.2.cloned.1.call-done = bf16[32,3072]{1,0:T(8,128)(2,1)} async-done(((bf16[128,3072]{1,0:T(8,128)(2,1)}), bf16[32,3072]{1,0:T(8,128)(2,1)}) %reduce-scatter.2.cloned.1.call-update) | async-done | bytes 196624 | tf_op jit(solution)/shard_map/reduce_scatter | solution.py:199
  186.2 4.6 %all-to-all-start.3 = ((bf16[4,8,3072]{2,1,0:T(8,128)(2,1)}), bf16[4,8,3072]{2,1,0:T(8,128)(2,1)S(1)}, u32[]{:S(2)}, u32[]{:S(2)}) async-start(bf16[4,8,3072]{2,1,0:T(8,128)(2,1)} %bitcast.71), calls=%async_computation.4 | async-start | bytes 393216 | tf_op jit(solution)/shard_map/all_to_all | solution.py:202
  190.9 0.1 copy.38
  190.9 0.1 select_reduce_fusion.1
  191.0 7.1 %all-to-all-done.3 = bf16[4,8,3072]{2,1,0:T(8,128)(2,1)S(1)} async-done(((bf16[4,8,3072]{2,1,0:T(8,128)(2,1)}), bf16[4,8,3072]{2,1,0:T(8,128)(2,1)S(1)}, u32[]{:S(2)}, u32[]{:S(2)}) %all-to-all-start.3) | async-done | bytes 196640 | tf_op jit(solution)/shard_map/all_to_all | solution.py:202
  198.2 0.8 fusion.7
  (46 shorter events, 0.5 us)
Async XLA Ops:
  6.5 154.9 %copy-start = (bf16[3072,8]{0,1:T(8,128)(2,1)S(1)}, bf16[3072,8]{0,1:T(8,128)(2,1)}, u32[]{:S(2)}) copy-start(bf16[3072,8]{0,1:T(8,128)(2,1)} %param.21) | copy-start | bytes 147460
  24.1 19.9 %copy-start.2 = (bf16[128,512]{1,0:T(8,128)(2,1)S(1)}, bf16[128,512]{1,0:T(8,128)(2,1)}, u32[]{:S(2)}) copy-start(bf16[128,512]{1,0:T(8,128)(2,1)} %param.16) | copy-start | bytes 393220
  24.1 20.0 %copy-start.3 = (bf16[128,512]{1,0:T(8,128)(2,1)S(1)}, bf16[128,512]{1,0:T(8,128)(2,1)}, u32[]{:S(2)}) copy-start(bf16[128,512]{1,0:T(8,128)(2,1)} %param.15) | copy-start | bytes 393220
  88.9 9.5 %copy-start.5 = (s32[1,8,2]{1,2,0:T(2,128)S(1)}, s32[1,8,2]{1,2,0:T(2,128)}, u32[]{:S(2)}) copy-start(s32[1,8,2]{1,2,0:T(2,128)} %param.25) | copy-start | bytes 196
  88.9 18.5 %copy-start.1 = (bf16[1,8,3072]{2,1,0:T(8,128)(2,1)S(1)}, bf16[1,8,3072]{2,1,0:T(8,128)(2,1)}, u32[]{:S(2)}) copy-start(bf16[1,8,3072]{2,1,0:T(8,128)(2,1)} %param.14) | copy-start | bytes 147460
  88.9 18.6 %copy-start.4 = (f32[3072]{0:T(1024)S(1)}, f32[3072]{0:T(1024)}, u32[]{:S(2)}) copy-start(f32[3072]{0:T(1024)} %param.18) | copy-start | bytes 36868
  93.2 10.8 %all-to-all-start = ((bf16[4,8,768]{2,1,0:T(8,128)(2,1)}), bf16[4,8,768]{2,1,0:T(8,128)(2,1)S(1)}, u32[]{:S(2)}, u32[]{:S(2)}) async-start(bf16[4,8,768]{2,1,0:T(8,128)(2,1)} %fusion.10), calls=%async_computation | async-start | bytes 98304 | tf_op jit(solution)/shard_map/all_to_all | solution.py:146
  104.1 8.6 %all-to-all-start.1 = ((s32[4,1,8]{2,1,0:T(1,128)}), s32[4,1,8]{2,1,0:T(1,128)S(1)}, u32[]{:S(2)}, u32[]{:S(2)}) async-start(s32[4,1,8]{2,1,0:T(1,128)} %bitcast.18), calls=%async_computation.1 | async-start | bytes 4096 | tf_op jit(solution)/shard_map/all_to_all | solution.py:182
  112.7 9.9 %all-to-all-start.2 = ((bf16[4,8,3072]{2,1,0:T(8,128)(2,1)}), bf16[4,8,3072]{2,1,0:T(8,128)(2,1)S(1)}, u32[]{:S(2)}, u32[]{:S(2)}) async-start(bf16[4,8,3072]{2,1,0:T(8,128)(2,1)} %fusion.5), calls=%async_computation.2 | async-start | bytes 393216 | tf_op jit(solution)/shard_map/all_to_all | solution.py:181
  116.1 70.2 %reduce-scatter.2.cloned.1.call-start = ((), (), s32[]{:S(2)}) async-start(), calls=%async_computation.5 | async-start | bytes 983040 | tf_op jit(solution)/shard_map/reduce_scatter | solution.py:199
  186.2 11.9 %all-to-all-start.3 = ((bf16[4,8,3072]{2,1,0:T(8,128)(2,1)}), bf16[4,8,3072]{2,1,0:T(8,128)(2,1)S(1)}, u32[]{:S(2)}, u32[]{:S(2)}) async-start(bf16[4,8,3072]{2,1,0:T(8,128)(2,1)} %bitcast.71), calls=%async_computation.4 | async-start | bytes 393216 | tf_op jit(solution)/shard_map/all_to_all | solution.py:202
Sparse Core Ops, SparseCore 0:
  161.6 24.5 reduce-scatter.1
where the time goes:
time: 206 us
  blocking collectives  85.9 us (42%)
  matrix products  40.7 us (20%)
  waiting for transfers between devices  39.8 us (19%)
  starting transfers between devices  16.3 us (8%)
  between operations  13.8 us (7%)
  other arithmetic  6.66 us (3%)
  local copies, waits for them, and re-layouts  2.66 us (1%)
    all_gather x3, blocking collectives, combined_all(): lax.all_gather(part.astype(kind), axis)  42 us
    reduce_scatter x1, waiting for transfers between devices, shards(): lax.psum_scatter(partial_out.astype(jnp.bfloat16), 'opt', scatter_dimensi...  24.3 us
    dot_general x1, matrix products, shards(): jnp.dot(hidden, down_weight, preferred_element_type=jnp.float32)  20 us
    all_gather x1, blocking collectives, shards(): row_piece = lax.all_gather(normed, 'ctx', axis=0, tiled=True)  15.5 us
    all_gather x1, blocking collectives, shards(): projected = lax.all_gather(rotated_tile, 'ctx', axis=1, tiled=True)  14.3 us
    dot_general x1, matrix products, shards(): gate_part = jnp.dot(pooled, gate_weight, preferred_element_type=jnp.float32)  9.97 us
    all_gather x1, blocking collectives, shards(): lax.all_gather(arrived, 'opt', axis=0, tiled=True)  8.88 us
    all_to_all x1, waiting for transfers between devices, shards(): lax.all_to_all(summed_back.reshape(ctx_count, slot_count, model_width).as...  7.12 us
  transfers between devices with their start and end apart: 5, of which 4 were waited for; matrix products, arithmetic and copies ran while one was open for 2% of the time, Pallas kernels for 0%

commit v1 on v0

--- a/solution.py
+++ b/solution.py
@@ -1,6 +1,8 @@
 import jax
 import jax.numpy as jnp
 from jax import lax
+from jax.experimental import pallas as pl
+from jax.experimental.pallas import tpu as pltpu
 from jax.sharding import PartitionSpec as P
 
 H = 24
@@ -92,7 +94,7 @@
     )
 
 
-def shards(
+def general_shards(
     options,
     cache_keys,
     cache_values,
@@ -217,6 +219,280 @@
     return layer_out[None]
 
 
+def gate_up_kernel(rows_ref, gate_ref, up_ref, hidden_ref):
+    gate = jnp.dot(rows_ref[...], gate_ref[...], preferred_element_type=jnp.float32)
+    up = jnp.dot(rows_ref[...], up_ref[...], preferred_element_type=jnp.float32)
+    hidden_ref[...] = (gate / (1.0 + jnp.exp(-gate)) * up).astype(hidden_ref.dtype)
+
+
+def down_kernel(hidden_ref, down_ref, out_ref):
+    out_ref[...] = jnp.dot(
+        hidden_ref[...], down_ref[...], preferred_element_type=jnp.float32
+    ).astype(out_ref.dtype)
+
+
+def tile_of(columns, most=1024):
+    tile = most
+    while columns % tile:
+        tile //= 2
+    return tile
+
+
+def expert_hidden(rows, gate_weight, up_weight):
+    count, depth = rows.shape
+    columns = gate_weight.shape[1]
+    tile = tile_of(columns)
+    weight_spec = pl.BlockSpec((depth, tile), lambda j: (0, j))
+    return pl.pallas_call(
+        gate_up_kernel,
+        out_shape=jax.ShapeDtypeStruct((count, columns), jnp.bfloat16),
+        grid=(columns // tile,),
+        in_specs=[pl.BlockSpec((count, depth), lambda j: (0, 0)), weight_spec, weight_spec],
+        out_specs=pl.BlockSpec((count, tile), lambda j: (0, j)),
+        cost_estimate=pl.CostEstimate(
+            flops=4 * count * depth * columns,
+            bytes_accessed=4 * depth * columns,
+            transcendentals=count * columns,
+        ),
+        name="expert_hidden",
+    )(rows, gate_weight, up_weight)
+
+
+def expert_down(hidden, down_weight, kind):
+    count, depth = hidden.shape
+    columns = down_weight.shape[1]
+    tile = tile_of(columns)
+    return pl.pallas_call(
+        down_kernel,
+        out_shape=jax.ShapeDtypeStruct((count, columns), kind),
+        grid=(columns // tile,),
+        in_specs=[
+            pl.BlockSpec((count, depth), lambda j: (0, 0)),
+            pl.BlockSpec((depth, tile), lambda j: (0, j)),
+        ],
+        out_specs=pl.BlockSpec((count, tile), lambda j: (0, j)),
+        cost_estimate=pl.CostEstimate(
+            flops=2 * count * depth * columns,
+            bytes_accessed=2 * depth * columns,
+            transcendentals=0,
+        ),
+        name="expert_down",
+    )(hidden, down_weight)
+
+
+def flip(x, axis, mask):
+    return lax.ppermute(x, axis, [(i, i ^ mask) for i in range(lax.axis_size(axis))])
+
+
+def by_index(index, variants):
+    chosen = variants[0]
+    for k in range(1, len(variants)):
+        chosen = jnp.where(index == k, variants[k], chosen)
+    return chosen
+
+
+def gathered(x, axis, index):
+    count = lax.axis_size(axis)
+    parts = [x] + [None] * (count - 1)
+    for mask in range(count - 1, 0, -1):
+        parts[mask] = flip(x, axis, mask)
+    return [by_index(index, [parts[place ^ here] for here in range(count)]) for place in range(count)]
+
+
+def head_plan(ctx_count, tile_heads):
+    per = H // ctx_count
+    wanted = [
+        [per * c + i for i in range(per)] + [H + c, H + KVH + c] for c in range(ctx_count)
+    ]
+    sends = {}
+    for dst in range(ctx_count):
+        for head in wanted[dst]:
+            sends.setdefault((head // tile_heads, dst), []).append(head)
+    return wanted, sends
+
+
+def exchange_heads(tile, axis, index):
+    count = lax.axis_size(axis)
+    tile_heads = tile.shape[1] // HD
+    wanted, sends = head_plan(count, tile_heads)
+
+    def head_of(block, k):
+        return block[:, k * HD : (k + 1) * HD]
+
+    arrived = {}
+    for shift in range(count - 1, 0, -1):
+        pairs = [(s, (s + shift) % count) for s in range(count) if (s, (s + shift) % count) in sends]
+        if not pairs:
+            continue
+        width = max(len(sends[pair]) for pair in pairs)
+        variants = []
+        for s in range(count):
+            heads = sends.get((s, (s + shift) % count), [])
+            local = [head - s * tile_heads for head in heads]
+            local = local + [0] * (width - len(local))
+            variants.append(jnp.concatenate([head_of(tile, k) for k in local], axis=1))
+        arrived[shift] = lax.ppermute(by_index(index, variants), axis, pairs)
+    results = []
+    for dst in range(count):
+        pieces = []
+        for head in wanted[dst]:
+            src = head // tile_heads
+            if src == dst:
+                pieces.append(head_of(tile, head - src * tile_heads))
+            else:
+                block = arrived[(dst - src) % count]
+                pieces.append(head_of(block, sends[(src, dst)].index(head)))
+        results.append(jnp.concatenate(pieces, axis=1))
+    return by_index(index, results)
+
+
+def fast_shards(
+    options,
+    cache_keys,
+    cache_values,
+    attention_gain,
+    expert_gain,
+    input_weight,
+    output_weight,
+    router_weight,
+    gate_weight,
+    up_weight,
+    down_weight,
+    routing,
+):
+    own_rows = options[0]
+    local_rows, model_width = own_rows.shape
+    ctx_count = lax.axis_size("ctx")
+    ctx_here = lax.axis_index("ctx")
+    opt_here = lax.axis_index("opt")
+    option_len = local_rows * ctx_count
+    passage = cache_keys.shape[0] * ctx_count
+    expert_count = router_weight.shape[1]
+    top_count = routing.shape[2]
+    group = H // KVH
+
+    extra = jnp.zeros((local_rows, HD), jnp.bfloat16)
+    extra = lax.dynamic_update_slice(extra, routing[0].astype(jnp.bfloat16), (0, 0))
+    packed = jnp.concatenate([own_rows, extra], axis=1)
+    packed = jnp.concatenate(gathered(packed, "ctx", ctx_here), axis=0)
+    all_rows = packed[:, :model_width]
+    chosen_ids = packed[:, model_width : model_width + top_count].astype(jnp.int32)
+
+    def passage_head(who):
+        return jnp.concatenate(
+            [
+                lax.dynamic_slice_in_dim(cache_keys, who * HD, HD, 1),
+                lax.dynamic_slice_in_dim(cache_values, who * HD, HD, 1),
+            ],
+            axis=1,
+        )
+
+    passage_parts = [passage_head(ctx_here)]
+    cache_seen, all_rows = lax.optimization_barrier(((cache_keys, cache_values), all_rows))
+    cache_keys, cache_values = cache_seen
+    for mask in range(ctx_count - 1, 0, -1):
+        passage_parts.append(flip(passage_head(ctx_here ^ mask), "ctx", mask))
+
+    normed = rms_scale(all_rows, attention_gain)
+    product = jnp.dot(normed, input_weight, preferred_element_type=jnp.float32)
+    first_head = ctx_here * (input_weight.shape[1] // HD)
+    rotated = rotate(product, first_head, passage + jnp.arange(option_len)).astype(jnp.bfloat16)
+    mine = exchange_heads(rotated, "ctx", ctx_here)
+
+    queries = mine[:, : group * HD].reshape(option_len, group, HD)
+    keys = jnp.concatenate([part[:, :HD] for part in passage_parts] + [mine[:, group * HD : (group + 1) * HD]], axis=0)
+    values = jnp.concatenate([part[:, HD:] for part in passage_parts] + [mine[:, (group + 1) * HD :]], axis=0)
+    scores = jnp.einsum("rgd,kd->grk", queries, keys, preferred_element_type=jnp.float32) * HD ** (-0.5)
+    key_index = jnp.arange(keys.shape[0])
+    visible = key_index[None, :] - passage <= jnp.arange(option_len)[:, None]
+    scores = jnp.where(visible, scores, -jnp.inf)
+    weights = jnp.exp(scores - jnp.max(scores, axis=-1, keepdims=True))
+    totals = jnp.sum(weights, axis=-1)
+    high = weights.astype(jnp.bfloat16)
+    low = (weights - high.astype(jnp.float32)).astype(jnp.bfloat16)
+    summed = jnp.einsum("grk,kd->grd", high, values, preferred_element_type=jnp.float32) + jnp.einsum(
+        "grk,kd->grd", low, values, preferred_element_type=jnp.float32
+    )
+    attention = (summed / totals[..., None]).transpose(1, 0, 2).reshape(option_len, group * HD)
+    attention = attention.astype(jnp.bfloat16)
+    attention = jnp.concatenate(gathered(attention, "ctx", ctx_here), axis=1)
+    out_width = output_weight.shape[1]
+    columns = jnp.dot(attention, output_weight, preferred_element_type=jnp.float32).astype(jnp.bfloat16)
+    own_columns = lax.dynamic_slice_in_dim(all_rows, ctx_here * out_width, out_width, 1)
+    mixed_columns = (own_columns.astype(jnp.float32) + columns.astype(jnp.float32)).astype(jnp.bfloat16)
+    mixed = jnp.concatenate(gathered(mixed_columns, "ctx", ctx_here), axis=1)
+
+    expert_in = rms_scale(mixed, expert_gain)
+    logits = jnp.dot(expert_in, router_weight, preferred_element_type=jnp.float32)
+    matches = chosen_ids[:, :, None] == jnp.arange(expert_count)[None, None, :]
+    picked = jnp.sum(jnp.where(matches, logits[:, None, :], 0.0), axis=-1)
+    gate_share = jax.nn.softmax(picked, axis=-1)
+    share_of = jnp.sum(jnp.where(matches, gate_share[:, :, None], 0.0), axis=1)
+    named = jnp.any(matches, axis=1)
+    earlier = jnp.arange(option_len)[None, :] < jnp.arange(option_len)[:, None]
+    rank = jnp.sum(jnp.where(earlier[:, :, None] & named[None, :, :], 1, 0), axis=1)
+    slots = MOST * ctx_count
+    half = opt_here // 2
+    own_expert = ctx_here * 2 + half
+    other_expert = ctx_here * 2 + 1 - half
+
+    def column(table, expert):
+        here = jnp.arange(expert_count) == expert
+        return jnp.sum(jnp.where(here[None, :], table, 0), axis=1)
+
+    def choice(expert):
+        taken = column(named.astype(jnp.int32), expert)
+        place = column(rank, expert)
+        hit = (place[None, :] == jnp.arange(slots)[:, None]) & (taken[None, :] == 1)
+        share = jnp.sum(jnp.where(hit, column(share_of, expert)[None, :], 0.0), axis=1)
+        return hit, share
+
+    own_hit, own_share = choice(own_expert)
+    other_hit, other_share = choice(other_expert)
+    hits = jnp.concatenate([own_hit, other_hit], axis=0).astype(jnp.bfloat16)
+    chosen_rows = jnp.dot(hits, expert_in, preferred_element_type=jnp.float32).astype(jnp.bfloat16)
+    own_slots, other_slots = chosen_rows[:slots], chosen_rows[slots:]
+    from_x = flip(other_slots, "opt", 2)
+    core_own = flip(own_slots, "opt", 1)
+    core_x = flip(from_x, "opt", 1)
+    expert_rows = jnp.concatenate([own_slots, from_x, core_own, core_x], axis=0)
+
+    hidden = expert_hidden(expert_rows, gate_weight, up_weight)
+    partial_out = expert_down(hidden, down_weight, jnp.float32)
+    from_core = flip(partial_out[2 * slots :].astype(jnp.bfloat16), "opt", 1)
+    total = partial_out[: 2 * slots] + from_core.astype(jnp.float32)
+    back = flip(total[slots:].astype(jnp.bfloat16), "opt", 2)
+    shares = jnp.concatenate([own_share, other_share], axis=0)
+    results = jnp.concatenate([total[:slots], back.astype(jnp.float32)], axis=0)
+    weighted = (results * shares[:, None]).astype(jnp.bfloat16)
+    spread = lax.dot_general(
+        hits, weighted, (((0,), (0,)), ((), ())), preferred_element_type=jnp.float32
+    )
+
+    def rows_of(table, who):
+        return lax.dynamic_slice_in_dim(table, who * local_rows, local_rows, 0)
+
+    expert_sum = rows_of(spread, ctx_here)
+    spread = spread.astype(jnp.bfloat16)
+    for mask in range(ctx_count - 1, 0, -1):
+        expert_sum = expert_sum + flip(rows_of(spread, ctx_here ^ mask), "ctx", mask).astype(jnp.float32)
+    layer_out = (rows_of(mixed, ctx_here).astype(jnp.float32) + expert_sum).astype(jnp.bfloat16)
+    return layer_out[None]
+
+
+def takes_fast(mesh, options, input_weight, output_weight, router_weight, gate_weight):
+    ctx_count, opt_count = mesh.shape["ctx"], mesh.shape["opt"]
+    devices = ctx_count * opt_count
+    return (
+        ctx_count == KVH
+        and opt_count == 4
+        and router_weight.shape[1] == 2 * ctx_count
+        and gate_weight.shape[1] == devices * (FF // 2)
+        and input_weight.shape[1] % (ctx_count * HD) == 0
+        and output_weight.shape[1] % (ctx_count * HD) == 0
+    )
+
+
 def solution(mesh):
     placed = (
         P(("parts", "opt"), "ctx", None),
@@ -232,10 +508,15 @@
         P(("ctx", "opt"), None),
         P(("parts", "opt"), "ctx", None),
     )
-    return jax.shard_map(
-        shards,
-        mesh=mesh,
-        in_specs=placed,
-        out_specs=P(("parts", "opt"), "ctx", None),
-        check_vma=False,
-    )
+
+    def layer(*args):
+        fast = takes_fast(mesh, args[0], args[5], args[6], args[7], args[8])
+        return jax.shard_map(
+            fast_shards if fast else general_shards,
+            mesh=mesh,
+            in_specs=placed,
+            out_specs=P(("parts", "opt"), "ctx", None),
+            check_vma=False,
+        )(*args)
+
+    return layer

time: 206 us -> 115 us (0.56)
  blocking collectives: 85.9 us -> 0 us
  matrix products: 40.7 us -> 8.96 us
  Pallas kernels: 0 us -> 30 us
  between operations: 13.8 us -> 0.53 us
  starting transfers between devices: 16.3 us -> 28.8 us
  waiting for transfers between devices: 39.8 us -> 35.1 us
    all_gather x7 -> x0, blocking collectives: 85.9 us -> none  [the longest x3 42 us: combined_all(): lax.all_gather(part.astype(kind), axis)]
    ppermute x0 -> x23, waiting for transfers between devices: none -> 35.1 us  [the longest x20 29 us: flip(): lax.ppermute(x, axis, [(i, i ^ mask) for i in range(lax.axis_size(axis))])]
    dot_general x9 -> x8, matrix products: 40.7 us -> 8.96 us  [the longest x1 4.04 us: fast_shards(): product = jnp.dot(normed, input_weight, preferred_element_type=jnp.float32)]
    pallas_call x0 -> x2, Pallas kernels: none -> 30 us  [the longest x1 18.9 us: expert_hidden(): pl.pallas_call(gate_up_kernel, out_shape=jax.ShapeDtypeStruct((count, col...]
    ppermute x0 -> x23, starting transfers between devices: none -> 28.8 us  [the longest x20 23.3 us: flip(): lax.ppermute(x, axis, [(i, i ^ mask) for i in range(lax.axis_size(axis))])]
    reduce_scatter x1 -> x0, waiting for transfers between devices: 24.3 us -> none  [shards(): lax.psum_scatter(partial_out.astype(jnp.bfloat16), 'opt', scatter_dimensi...]
    all_to_all x4 -> x0, starting transfers between devices: 16.2 us -> none  [the longest x1 5.04 us: shards(): lax.all_to_all(columns, 'ctx', split_axis=0, concat_axis=1, tiled=True)]
    all_to_all x4 -> x0, waiting for transfers between devices: 15.4 us -> none  [the longest x1 7.12 us: shards(): lax.all_to_all(summed_back.reshape(ctx_count, slot_count, model_width).as...]
  transfers between devices with their start and end apart: 5 -> 23, of which waited for: 4 -> 15; matrix products, arithmetic and copies ran while one was open for 2% -> 2% of each run, Pallas kernels for 0% -> 0%
where the time goes in v1:
time: 115 us; the launch traced here: 114 us
  waiting for transfers between devices  35.1 us (31%)
  Pallas kernels  30 us (26%)
  starting transfers between devices  28.8 us (25%)
  matrix products  8.96 us (8%)
  other arithmetic  7.76 us (7%)
  local copies, waits for them, and re-layouts  2.89 us (3%)
    ppermute x20, waiting for transfers between devices, flip(): lax.ppermute(x, axis, [(i, i ^ mask) for i in range(lax.axis_size(axis))])  29 us
    ppermute x20, starting transfers between devices, flip(): lax.ppermute(x, axis, [(i, i ^ mask) for i in range(lax.axis_size(axis))])  23.3 us
    pallas_call x1, Pallas kernels, expert_hidden(): pl.pallas_call(gate_up_kernel, out_shape=jax.ShapeDtypeStruct((count, col...  18.9 us
    pallas_call x1, Pallas kernels, expert_down(): pl.pallas_call(down_kernel, out_shape=jax.ShapeDtypeStruct((count, column...  11.1 us
    ppermute x3, waiting for transfers between devices, exchange_heads(): arrived[shift] = lax.ppermute(by_index(index, variants), axis, pairs)  6.18 us
    ppermute x3, starting transfers between devices, exchange_heads(): arrived[shift] = lax.ppermute(by_index(index, variants), axis, pairs)  5.5 us
    dot_general x1, matrix products, fast_shards(): product = jnp.dot(normed, input_weight, preferred_element_type=jnp.float32)  4.04 us
    dot_general x1, matrix products, fast_shards(): jnp.dot(attention, output_weight, preferred_element_type=jnp.float32)  3.26 us
  transfers between devices with their start and end apart: 23, of which 15 were waited for; matrix products, arithmetic and copies ran while one was open for 2% of the time, Pallas kernels for 0%

profile of v1, /device:TPU:0, one launch (start us, length us, event | category | flops | bytes accessed | tf_op | source)
XLA Modules:
  0.0 114.1 jit_solution(10035980338546714949)
XLA Ops:
  0.0 0.7 convert_bitcast_fusion
  0.7 0.1 copy.56
  0.8 0.8 fusion.39
  1.6 3.1 %collective-permute-start.2 = (bf16[8,3200]{1,0:T(8,128)(2,1)S(1)}, bf16[8,3200]{1,0:T(8,128)(2,1)S(1)}, u32[]{:S(2)}, u32[]{:S(2)}) collective-permute-start(bf16[8,3200]{1,0:T(8,128)(2,1)S(1)} %fusion.39), channel_id=1, source_target_pairs={{0,4},{4,0},{8,12},{12,8},{1,5},{5,1},{9,13},{13,9},{2,6},{6,2},{1... | collective-permute-start | bytes 153608 | tf_op jit(solution)/shard_map/ppermute | solution.py:284
  4.7 2.6 %collective-permute-start.1 = (bf16[8,3200]{1,0:T(8,128)(2,1)S(1)}, bf16[8,3200]{1,0:T(8,128)(2,1)S(1)}, u32[]{:S(2)}, u32[]{:S(2)}) collective-permute-start(bf16[8,3200]{1,0:T(8,128)(2,1)S(1)} %fusion.39), channel_id=1, source_target_pairs={{0,8},{4,12},{8,0},{12,4},{1,9},{5,13},{9,1},{13,5},{2,10},{6,14},... | collective-permute-start | bytes 153608 | tf_op jit(solution)/shard_map/ppermute | solution.py:284
  7.4 0.1 multiply_cosine_fusion
  7.5 0.8 constant_dynamic-update-slice_fusion.15
  8.4 0.1 broadcast_in_dim.152
  8.5 2.1 %collective-permute-done.1 = bf16[8,3200]{1,0:T(8,128)(2,1)S(1)} collective-permute-done((bf16[8,3200]{1,0:T(8,128)(2,1)S(1)}, bf16[8,3200]{1,0:T(8,128)(2,1)S(1)}, u32[]{:S(2)}, u32[]{:S(2)}) %collective-permute-start.1) | collective-permute-done | bytes 51232 | tf_op jit(solution)/shard_map/ppermute | solution.py:284
  10.7 2.5 %collective-permute-done = bf16[8,3200]{1,0:T(8,128)(2,1)S(1)} collective-permute-done((bf16[8,3200]{1,0:T(8,128)(2,1)S(1)}, bf16[8,3200]{1,0:T(8,128)(2,1)S(1)}, u32[]{:S(2)}, u32[]{:S(2)}) %collective-permute-start) | collective-permute-done | bytes 51232 | tf_op jit(solution)/shard_map/ppermute | solution.py:284
  13.2 0.9 select_select_fusion.3
  14.1 0.2 fusion.9
  14.3 4.0 %fusion.23 = f32[32,1024]{1,0:T(8,128)S(1)} fusion(bf16[3072,1024]{1,0:T(8,128)(2,1)} %param.17, bf16[32,3072]{1,0:T(8,128)(2,1)S(1)} %slice.210, f32[3072]{0:T(1024)} %param.15, f32[32]{0:T(128)S(1)} %add_rsqrt_fusion.1), kind=kOutput, calls=%fused_computation.37 | convolution fusion | flops 201719808 | bytes 6631552 | tf_op jit(solution)/shard_map/dot_general | solution.py:397
  18.3 0.2 reshape.170
  18.5 0.4 multiply_subtract_fusion
  18.9 0.4 pad_maximum_fusion.1
  19.3 0.1 stack.8
  19.5 0.1 copy.55
  19.6 0.6 select_reduce_fusion
  20.3 0.1 fusion.50
  20.5 0.9 collective-permute-start.3
  21.6 0.7 collective-permute-start.8
  22.3 0.7 collective-permute-start.7
  23.0 4.2 %collective-permute-start.6 = (bf16[32,768]{1,0:T(8,128)(2,1)S(1)}, bf16[32,768]{1,0:T(8,128)(2,1)S(1)}, u32[]{:S(2)}, u32[]{:S(2)}) collective-permute-start(bf16[32,768]{1,0:T(8,128)(2,1)S(1)} %get-tuple-element.55), channel_id=1, source_target_pairs={{0,4},{4,8},{8,12},{12,0},{1,5},{5,9},{9,13},{13,1},{2,6},{6,10},{... | collective-permute-start | bytes 147464 | tf_op jit(solution)/shard_map/ppermute | solution.py:334
  27.2 6.2 %collective-permute-done.6 = bf16[32,768]{1,0:T(8,128)(2,1)S(1)} collective-permute-done((bf16[32,768]{1,0:T(8,128)(2,1)S(1)}, bf16[32,768]{1,0:T(8,128)(2,1)S(1)}, u32[]{:S(2)}, u32[]{:S(2)}) %collective-permute-start.6) | collective-permute-done | bytes 49184 | tf_op jit(solution)/shard_map/ppermute | solution.py:334
  33.5 5.1 %collective-permute-done.5 = bf16[128,256]{1,0:T(8,128)(2,1)S(1)} collective-permute-done((bf16[128,256]{1,0:T(8,128)(2,1)S(1)}, bf16[128,256]{1,0:T(8,128)(2,1)S(1)}, u32[]{:S(2)}, u32[]{:S(2)}) %collective-permute-start.5) | collective-permute-done | bytes 65568 | tf_op jit(solution)/shard_map/ppermute | solution.py:284
  38.6 0.3 fusion.63
  39.0 0.2 fusion.16
  39.2 0.3 fusion.20
  39.5 0.3 fusion.8
  39.9 2.1 %collective-permute-start.10 = (bf16[32,768]{1,0:T(8,128)(2,1)S(1)}, bf16[32,768]{1,0:T(8,128)(2,1)S(1)}, u32[]{:S(2)}, u32[]{:S(2)}) collective-permute-start(bf16[32,768]{1,0:T(8,128)(2,1)S(1)} %bitcast.56), channel_id=1, source_target_pairs={{0,8},{4,12},{8,0},{12,4},{1,9},{5,13},{9,1},{13,5},{2,10},{6,14},... | collective-permute-start | bytes 147464 | tf_op jit(solution)/shard_map/ppermute | solution.py:284
  42.0 2.2 %collective-permute-start.9 = (bf16[32,768]{1,0:T(8,128)(2,1)S(1)}, bf16[32,768]{1,0:T(8,128)(2,1)S(1)}, u32[]{:S(2)}, u32[]{:S(2)}) collective-permute-start(bf16[32,768]{1,0:T(8,128)(2,1)S(1)} %bitcast.57), channel_id=1, source_target_pairs={{0,12},{4,8},{8,4},{12,0},{1,13},{5,9},{9,5},{13,1},{2,14},{6,10},... | collective-permute-start | bytes 147464 | tf_op jit(solution)/shard_map/ppermute | solution.py:284
  44.3 0.7 collective-permute-done.10
  44.9 3.3 %collective-permute-done.9 = bf16[32,768]{1,0:T(8,128)(2,1)S(1)} collective-permute-done((bf16[32,768]{1,0:T(8,128)(2,1)S(1)}, bf16[32,768]{1,0:T(8,128)(2,1)S(1)}, u32[]{:S(2)}, u32[]{:S(2)}) %collective-permute-start.9) | collective-permute-done | bytes 49184 | tf_op jit(solution)/shard_map/ppermute | solution.py:284
  48.2 3.3 %fusion.6 = bf16[32,768]{1,0:T(8,128)(2,1)S(1)} fusion(bf16[3072,768]{1,0:T(8,128)(2,1)} %param.18, bf16[32,768]{1,0:T(8,128)(2,1)S(1)} %get-tuple-element.37, bf16[32,768]{1,0:T(8,128)(2,1)S(1)} %get-tuple-element.38, bf16[32,768]{1,0:T(8,128)(2,1)S(1)} %get-tuple-element.39, bf16[32,768]{1,0:T(8,128)(2,1)S(1)} %get-tuple-element.36, ...), kind=kOutput, calls=%fused_computation.10 | convolution fusion | flops 151904256 | bytes 5013508 | tf_op jit(solution)/shard_map/dot_general | solution.py:420
  51.6 2.5 %collective-permute-start.13 = (bf16[32,768]{1,0:T(8,128)(2,1)S(1)}, bf16[32,768]{1,0:T(8,128)(2,1)S(1)}, u32[]{:S(2)}, u32[]{:S(2)}) collective-permute-start(bf16[32,768]{1,0:T(8,128)(2,1)S(1)} %fusion.6), channel_id=1, source_target_pairs={{0,8},{4,12},{8,0},{12,4},{1,9},{5,13},{9,1},{13,5},{2,10},{6,14},... | collective-permute-start | bytes 147464 | tf_op jit(solution)/shard_map/ppermute | solution.py:284
  54.1 1.8 %collective-permute-start.12 = (bf16[32,768]{1,0:T(8,128)(2,1)S(1)}, bf16[32,768]{1,0:T(8,128)(2,1)S(1)}, u32[]{:S(2)}, u32[]{:S(2)}) collective-permute-start(bf16[32,768]{1,0:T(8,128)(2,1)S(1)} %fusion.6), channel_id=1, source_target_pairs={{0,12},{4,8},{8,4},{12,0},{1,13},{5,9},{9,5},{13,1},{2,14},{6,10},... | collective-permute-start | bytes 147464 | tf_op jit(solution)/shard_map/ppermute | solution.py:284
  56.0 0.7 collective-permute-done.13
  56.6 3.4 %collective-permute-done.12 = bf16[32,768]{1,0:T(8,128)(2,1)S(1)} collective-permute-done((bf16[32,768]{1,0:T(8,128)(2,1)S(1)}, bf16[32,768]{1,0:T(8,128)(2,1)S(1)}, u32[]{:S(2)}, u32[]{:S(2)}) %collective-permute-start.12) | collective-permute-done | bytes 49184 | tf_op jit(solution)/shard_map/ppermute | solution.py:284
  60.0 0.2 fusion.12
  60.2 0.2 fusion.40
  60.5 0.3 convolution_convert_fusion
  60.8 1.6 %collective-permute-start.15 = (bf16[16,3072]{1,0:T(8,128)(2,1)S(1)}, bf16[16,3072]{1,0:T(8,128)(2,1)S(1)}, u32[]{:S(2)}, u32[]{:S(2)}) collective-permute-start(bf16[16,3072]{1,0:T(8,128)(2,1)S(1)} %get-tuple-element.31), channel_id=1, source_target_pairs={{0,2},{1,3},{2,0},{3,1},{4,6},{5,7},{6,4},{7,5},{8,10},{9,11},{10,... | collective-permute-start | bytes 294920 | tf_op jit(solution)/shard_map/ppermute | solution.py:284
  62.4 3.1 %collective-permute-done.15 = bf16[16,3072]{1,0:T(8,128)(2,1)S(1)} collective-permute-done((bf16[16,3072]{1,0:T(8,128)(2,1)S(1)}, bf16[16,3072]{1,0:T(8,128)(2,1)S(1)}, u32[]{:S(2)}, u32[]{:S(2)}) %collective-permute-start.15) | collective-permute-done | bytes 98336 | tf_op jit(solution)/shard_map/ppermute | solution.py:284
  65.5 0.1 select_reduce_fusion.6
  65.6 1.2 %collective-permute-done.17 = bf16[16,3072]{1,0:T(8,128)(2,1)S(1)} collective-permute-done((bf16[16,3072]{1,0:T(8,128)(2,1)S(1)}, bf16[16,3072]{1,0:T(8,128)(2,1)S(1)}, u32[]{:S(2)}, u32[]{:S(2)}) %collective-permute-start.17) | collective-permute-done | bytes 98336 | tf_op jit(solution)/shard_map/ppermute | solution.py:284
  66.8 0.8 pad_maximum_fusion.rows_ref
  67.6 18.9 %expert_hidden.1.hidden_ref = bf16[64,4096]{1,0:T(8,128)(2,1)} custom-call(bf16[64,3072]{1,0:T(8,128)(2,1)} %pad_maximum_fusion.rows_ref, bf16[3072,4096]{1,0:T(8,128)(2,1)} %gate_ref.1, bf16[3072,4096]{1,0:T(8,128)(2,1)} %up_ref.1), custom_call_target="tpu_custom_call" | custom-call | flops 3221225472 | bytes 50331648 | tf_op jit(solution)/shard_map/expert_hidden/pallas_call | solution.py:246
  86.5 11.1 %expert_down.1 = f32[64,3072]{1,0:T(8,128)} custom-call(bf16[64,4096]{1,0:T(8,128)(2,1)} %expert_hidden.1.hidden_ref, bf16[4096,3072]{1,0:T(8,128)(2,1)} %down_ref.1), custom_call_target="tpu_custom_call" | custom-call | flops 1610612736 | bytes 25165824 | tf_op jit(solution)/shard_map/expert_down/pallas_call | solution.py:265
  97.6 1.0 slice.274
  98.6 0.2 collective-permute-start.18
  98.8 0.1 select_reduce_fusion.1
  98.9 0.1 select_reduce_fusion.2
  99.0 1.1 collective-permute-done.18
  100.1 1.0 slice_add_fusion
  101.2 1.6 %collective-permute-start.19 = (bf16[16,3072]{1,0:T(8,128)(2,1)S(1)}, bf16[16,3072]{1,0:T(8,128)(2,1)S(1)}, u32[]{:S(2)}, u32[]{:S(2)}) collective-permute-start(bf16[16,3072]{1,0:T(8,128)(2,1)S(1)} %slice.275), channel_id=1, source_target_pairs={{0,2},{1,3},{2,0},{3,1},{4,6},{5,7},{6,4},{7,5},{8,10},{9,11},{10,... | collective-permute-start | bytes 294920 | tf_op jit(solution)/shard_map/ppermute | solution.py:284
  102.8 3.3 %collective-permute-done.19 = bf16[16,3072]{1,0:T(8,128)(2,1)S(1)} collective-permute-done((bf16[16,3072]{1,0:T(8,128)(2,1)S(1)}, bf16[16,3072]{1,0:T(8,128)(2,1)S(1)}, u32[]{:S(2)}, u32[]{:S(2)}) %collective-permute-start.19) | collective-permute-done | bytes 98336 | tf_op jit(solution)/shard_map/ppermute | solution.py:284
  106.1 0.3 fusion.64
  106.4 1.9 %collective-permute-start.20 = (bf16[8,3072]{1,0:T(8,128)(2,1)S(1)}, bf16[8,3072]{1,0:T(8,128)(2,1)S(1)}, u32[]{:S(2)}, u32[]{:S(2)}) collective-permute-start(bf16[8,3072]{1,0:T(8,128)(2,1)S(1)} %get-tuple-element.27), channel_id=1, source_target_pairs={{0,12},{4,8},{8,4},{12,0},{1,13},{5,9},{9,5},{13,1},{2,14},{6,10},... | collective-permute-start | bytes 147464 | tf_op jit(solution)/shard_map/ppermute | solution.py:284
  108.3 2.5 %collective-permute-start.21 = (bf16[8,3072]{1,0:T(8,128)(2,1)S(1)}, bf16[8,3072]{1,0:T(8,128)(2,1)S(1)}, u32[]{:S(2)}, u32[]{:S(2)}) collective-permute-start(bf16[8,3072]{1,0:T(8,128)(2,1)S(1)} %get-tuple-element.29), channel_id=1, source_target_pairs={{0,8},{4,12},{8,0},{12,4},{1,9},{5,13},{9,1},{13,5},{2,10},{6,14},... | collective-permute-start | bytes 147464 | tf_op jit(solution)/shard_map/ppermute | solution.py:284
  110.8 1.9 %collective-permute-done.20 = bf16[8,3072]{1,0:T(8,128)(2,1)S(1)} collective-permute-done((bf16[8,3072]{1,0:T(8,128)(2,1)S(1)}, bf16[8,3072]{1,0:T(8,128)(2,1)S(1)}, u32[]{:S(2)}, u32[]{:S(2)}) %collective-permute-start.20) | collective-permute-done | bytes 49184 | tf_op jit(solution)/shard_map/ppermute | solution.py:284
  112.7 0.3 collective-permute-done.22
  113.0 0.5 collective-permute-done.21
  113.4 0.7 fusion.43
  (83 shorter events, 1.2 us)
Async XLA Ops:
  0.0 60.2 %copy-start = (bf16[3072,8]{0,1:T(8,128)(2,1)S(1)}, bf16[3072,8]{0,1:T(8,128)(2,1)}, u32[]{:S(2)}) copy-start(bf16[3072,8]{0,1:T(8,128)(2,1)} %param.19) | copy-start | bytes 147460
  0.0 20.4 %copy-start.3 = (bf16[128,512]{1,0:T(8,128)(2,1)S(1)}, bf16[128,512]{1,0:T(8,128)(2,1)}, u32[]{:S(2)}) copy-start(bf16[128,512]{1,0:T(8,128)(2,1)} %param.14) | copy-start | bytes 393220
  0.0 20.4 %copy-start.2 = (bf16[128,512]{1,0:T(8,128)(2,1)S(1)}, bf16[128,512]{1,0:T(8,128)(2,1)}, u32[]{:S(2)}) copy-start(bf16[128,512]{1,0:T(8,128)(2,1)} %param.13) | copy-start | bytes 393220
  1.6 6.9 %collective-permute-start.2 = (bf16[8,3200]{1,0:T(8,128)(2,1)S(1)}, bf16[8,3200]{1,0:T(8,128)(2,1)S(1)}, u32[]{:S(2)}, u32[]{:S(2)}) collective-permute-start(bf16[8,3200]{1,0:T(8,128)(2,1)S(1)} %fusion.39), channel_id=1, source_target_pairs={{0,4},{4,0},{8,12},{12,8},{1,5},{5,1},{9,13},{13,9},{2,6},{6,2},{1... | collective-permute-start | bytes 153608 | tf_op jit(solution)/shard_map/ppermute | solution.py:284
  4.7 6.0 %collective-permute-start.1 = (bf16[8,3200]{1,0:T(8,128)(2,1)S(1)}, bf16[8,3200]{1,0:T(8,128)(2,1)S(1)}, u32[]{:S(2)}, u32[]{:S(2)}) collective-permute-start(bf16[8,3200]{1,0:T(8,128)(2,1)S(1)} %fusion.39), channel_id=1, source_target_pairs={{0,8},{4,12},{8,0},{12,4},{1,9},{5,13},{9,1},{13,5},{2,10},{6,14},... | collective-permute-start | bytes 153608 | tf_op jit(solution)/shard_map/ppermute | solution.py:284
  7.3 5.9 %collective-permute-start = (bf16[8,3200]{1,0:T(8,128)(2,1)S(1)}, bf16[8,3200]{1,0:T(8,128)(2,1)S(1)}, u32[]{:S(2)}, u32[]{:S(2)}) collective-permute-start(bf16[8,3200]{1,0:T(8,128)(2,1)S(1)} %fusion.39), channel_id=1, source_target_pairs={{0,12},{4,8},{8,4},{12,0},{1,13},{5,9},{9,5},{13,1},{2,14},{6,10},... | collective-permute-start | bytes 153608 | tf_op jit(solution)/shard_map/ppermute | solution.py:284
  18.9 41.3 %copy-start.4 = (f32[3072]{0:T(1024)S(1)}, f32[3072]{0:T(1024)}, u32[]{:S(2)}) copy-start(f32[3072]{0:T(1024)} %param.16) | copy-start | bytes 36868
  20.5 13.0 %collective-permute-start.3 = (bf16[128,256]{1,0:T(8,128)(2,1)S(1)}, bf16[128,256]{1,0:T(8,128)(2,1)S(1)}, u32[]{:S(2)}, u32[]{:S(2)}) collective-permute-start(bf16[128,256]{1,0:T(8,128)(2,1)S(1)} %pad_maximum_fusion.4), channel_id=1, source_target_pairs={{0,12},{4,8},{8,4},{12,0},{1,13},{5,9},{9,5},{13,1},{2,14},{6,10},... | collective-permute-start | bytes 196616 | tf_op jit(solution)/shard_map/ppermute | solution.py:284
  21.4 12.1 %collective-permute-start.4 = (bf16[128,256]{1,0:T(8,128)(2,1)S(1)}, bf16[128,256]{1,0:T(8,128)(2,1)S(1)}, u32[]{:S(2)}, u32[]{:S(2)}) collective-permute-start(bf16[128,256]{1,0:T(8,128)(2,1)S(1)} %pad_maximum_fusion.5), channel_id=1, source_target_pairs={{0,8},{4,12},{8,0},{12,4},{1,9},{5,13},{9,1},{13,5},{2,10},{6,14},... | collective-permute-start | bytes 196616 | tf_op jit(solution)/shard_map/ppermute | solution.py:284
  21.6 11.8 %collective-permute-start.8 = (bf16[32,256]{1,0:T(8,128)(2,1)S(1)}, bf16[32,256]{1,0:T(8,128)(2,1)S(1)}, u32[]{:S(2)}, u32[]{:S(2)}) collective-permute-start(bf16[32,256]{1,0:T(8,128)(2,1)S(1)} %get-tuple-element.73), channel_id=1, source_target_pairs={{12,4},{13,5},{14,6},{15,7},{28,20},{29,21},{30,22},{31,23}} | collective-permute-start | bytes 49160 | tf_op jit(solution)/shard_map/ppermute | solution.py:334
  22.3 11.1 %collective-permute-start.7 = (bf16[32,256]{1,0:T(8,128)(2,1)S(1)}, bf16[32,256]{1,0:T(8,128)(2,1)S(1)}, u32[]{:S(2)}, u32[]{:S(2)}) collective-permute-start(bf16[32,256]{1,0:T(8,128)(2,1)S(1)} %get-tuple-element.74), channel_id=1, source_target_pairs={{12,8},{13,9},{14,10},{15,11},{28,24},{29,25},{30,26},{31,27}} | collective-permute-start | bytes 49160 | tf_op jit(solution)/shard_map/ppermute | solution.py:334
  23.0 10.4 %collective-permute-start.6 = (bf16[32,768]{1,0:T(8,128)(2,1)S(1)}, bf16[32,768]{1,0:T(8,128)(2,1)S(1)}, u32[]{:S(2)}, u32[]{:S(2)}) collective-permute-start(bf16[32,768]{1,0:T(8,128)(2,1)S(1)} %get-tuple-element.55), channel_id=1, source_target_pairs={{0,4},{4,8},{8,12},{12,0},{1,5},{5,9},{9,13},{13,1},{2,6},{6,10},{... | collective-permute-start | bytes 147464 | tf_op jit(solution)/shard_map/ppermute | solution.py:334
  33.4 5.2 %collective-permute-start.5 = (bf16[128,256]{1,0:T(8,128)(2,1)S(1)}, bf16[128,256]{1,0:T(8,128)(2,1)S(1)}, u32[]{:S(2)}, u32[]{:S(2)}) collective-permute-start(bf16[128,256]{1,0:T(8,128)(2,1)S(1)} %pad_maximum_fusion.6), channel_id=1, source_target_pairs={{0,4},{4,0},{8,12},{12,8},{1,5},{5,1},{9,13},{13,9},{2,6},{6,2},{1... | collective-permute-start | bytes 196616 | tf_op jit(solution)/shard_map/ppermute | solution.py:284
  39.8 4.5 %collective-permute-start.11 = (bf16[32,768]{1,0:T(8,128)(2,1)S(1)}, bf16[32,768]{1,0:T(8,128)(2,1)S(1)}, u32[]{:S(2)}, u32[]{:S(2)}) collective-permute-start(bf16[32,768]{1,0:T(8,128)(2,1)S(1)} %bitcast.55), channel_id=1, source_target_pairs={{0,4},{4,0},{8,12},{12,8},{1,5},{5,1},{9,13},{13,9},{2,6},{6,2},{1... | collective-permute-start | bytes 147464 | tf_op jit(solution)/shard_map/ppermute | solution.py:284
  39.9 5.1 %collective-permute-start.10 = (bf16[32,768]{1,0:T(8,128)(2,1)S(1)}, bf16[32,768]{1,0:T(8,128)(2,1)S(1)}, u32[]{:S(2)}, u32[]{:S(2)}) collective-permute-start(bf16[32,768]{1,0:T(8,128)(2,1)S(1)} %bitcast.56), channel_id=1, source_target_pairs={{0,8},{4,12},{8,0},{12,4},{1,9},{5,13},{9,1},{13,5},{2,10},{6,14},... | collective-permute-start | bytes 147464 | tf_op jit(solution)/shard_map/ppermute | solution.py:284
  42.0 6.2 %collective-permute-start.9 = (bf16[32,768]{1,0:T(8,128)(2,1)S(1)}, bf16[32,768]{1,0:T(8,128)(2,1)S(1)}, u32[]{:S(2)}, u32[]{:S(2)}) collective-permute-start(bf16[32,768]{1,0:T(8,128)(2,1)S(1)} %bitcast.57), channel_id=1, source_target_pairs={{0,12},{4,8},{8,4},{12,0},{1,13},{5,9},{9,5},{13,1},{2,14},{6,10},... | collective-permute-start | bytes 147464 | tf_op jit(solution)/shard_map/ppermute | solution.py:284
  51.5 4.5 %collective-permute-start.14 = (bf16[32,768]{1,0:T(8,128)(2,1)S(1)}, bf16[32,768]{1,0:T(8,128)(2,1)S(1)}, u32[]{:S(2)}, u32[]{:S(2)}) collective-permute-start(bf16[32,768]{1,0:T(8,128)(2,1)S(1)} %fusion.6), channel_id=1, source_target_pairs={{0,4},{4,0},{8,12},{12,8},{1,5},{5,1},{9,13},{13,9},{2,6},{6,2},{1... | collective-permute-start | bytes 147464 | tf_op jit(solution)/shard_map/ppermute | solution.py:284
  51.6 5.1 %collective-permute-start.13 = (bf16[32,768]{1,0:T(8,128)(2,1)S(1)}, bf16[32,768]{1,0:T(8,128)(2,1)S(1)}, u32[]{:S(2)}, u32[]{:S(2)}) collective-permute-start(bf16[32,768]{1,0:T(8,128)(2,1)S(1)} %fusion.6), channel_id=1, source_target_pairs={{0,8},{4,12},{8,0},{12,4},{1,9},{5,13},{9,1},{13,5},{2,10},{6,14},... | collective-permute-start | bytes 147464 | tf_op jit(solution)/shard_map/ppermute | solution.py:284
  54.1 5.9 %collective-permute-start.12 = (bf16[32,768]{1,0:T(8,128)(2,1)S(1)}, bf16[32,768]{1,0:T(8,128)(2,1)S(1)}, u32[]{:S(2)}, u32[]{:S(2)}) collective-permute-start(bf16[32,768]{1,0:T(8,128)(2,1)S(1)} %fusion.6), channel_id=1, source_target_pairs={{0,12},{4,8},{8,4},{12,0},{1,13},{5,9},{9,5},{13,1},{2,14},{6,10},... | collective-permute-start | bytes 147464 | tf_op jit(solution)/shard_map/ppermute | solution.py:284
  60.8 4.7 %collective-permute-start.15 = (bf16[16,3072]{1,0:T(8,128)(2,1)S(1)}, bf16[16,3072]{1,0:T(8,128)(2,1)S(1)}, u32[]{:S(2)}, u32[]{:S(2)}) collective-permute-start(bf16[16,3072]{1,0:T(8,128)(2,1)S(1)} %get-tuple-element.31), channel_id=1, source_target_pairs={{0,2},{1,3},{2,0},{3,1},{4,6},{5,7},{6,4},{7,5},{8,10},{9,11},{10,... | collective-permute-start | bytes 294920 | tf_op jit(solution)/shard_map/ppermute | solution.py:284
  62.4 3.2 %collective-permute-start.16 = (bf16[16,3072]{1,0:T(8,128)(2,1)S(1)}, bf16[16,3072]{1,0:T(8,128)(2,1)S(1)}, u32[]{:S(2)}, u32[]{:S(2)}) collective-permute-start(bf16[16,3072]{1,0:T(8,128)(2,1)S(1)} %get-tuple-element.30), channel_id=1, source_target_pairs={{0,1},{1,0},{2,3},{3,2},{4,5},{5,4},{6,7},{7,6},{8,9},{9,8},{10,11... | collective-permute-start | bytes 294920 | tf_op jit(solution)/shard_map/ppermute | solution.py:284
  65.5 1.3 %collective-permute-start.17 = (bf16[16,3072]{1,0:T(8,128)(2,1)S(1)}, bf16[16,3072]{1,0:T(8,128)(2,1)S(1)}, u32[]{:S(2)}, u32[]{:S(2)}) collective-permute-start(bf16[16,3072]{1,0:T(8,128)(2,1)S(1)} %collective-permute-done.15), channel_id=1, source_target_pairs={{0,1},{1,0},{2,3},{3,2},{4,5},{5,4},{6,7},{7,6},{8,9},{9,8},{10,11... | collective-permute-start | bytes 294920 | tf_op jit(solution)/shard_map/ppermute | solution.py:284
  86.5 27.6 %copy-start.1 = (bf16[3072,8]{0,1:T(8,128)(2,1)S(1)}, bf16[3072,8]{0,1:T(8,128)(2,1)}, u32[]{:S(2)}) copy-start(bf16[3072,8]{0,1:T(8,128)(2,1)} %param.19) | copy-start | bytes 147460
  98.6 1.5 %collective-permute-start.18 = (bf16[32,3072]{1,0:T(8,128)(2,1)S(1)}, bf16[32,3072]{1,0:T(8,128)(2,1)S(1)}, u32[]{:S(2)}, u32[]{:S(2)}) collective-permute-start(bf16[32,3072]{1,0:T(8,128)(2,1)S(1)} %slice.274), channel_id=1, source_target_pairs={{0,1},{1,0},{2,3},{3,2},{4,5},{5,4},{6,7},{7,6},{8,9},{9,8},{10,11... | collective-permute-start | bytes 589832 | tf_op jit(solution)/shard_map/ppermute | solution.py:284
  101.2 4.9 %collective-permute-start.19 = (bf16[16,3072]{1,0:T(8,128)(2,1)S(1)}, bf16[16,3072]{1,0:T(8,128)(2,1)S(1)}, u32[]{:S(2)}, u32[]{:S(2)}) collective-permute-start(bf16[16,3072]{1,0:T(8,128)(2,1)S(1)} %slice.275), channel_id=1, source_target_pairs={{0,2},{1,3},{2,0},{3,1},{4,6},{5,7},{6,4},{7,5},{8,10},{9,11},{10,... | collective-permute-start | bytes 294920 | tf_op jit(solution)/shard_map/ppermute | solution.py:284
  106.4 6.3 %collective-permute-start.20 = (bf16[8,3072]{1,0:T(8,128)(2,1)S(1)}, bf16[8,3072]{1,0:T(8,128)(2,1)S(1)}, u32[]{:S(2)}, u32[]{:S(2)}) collective-permute-start(bf16[8,3072]{1,0:T(8,128)(2,1)S(1)} %get-tuple-element.27), channel_id=1, source_target_pairs={{0,12},{4,8},{8,4},{12,0},{1,13},{5,9},{9,5},{13,1},{2,14},{6,10},... | collective-permute-start | bytes 147464 | tf_op jit(solution)/shard_map/ppermute | solution.py:284
  108.3 4.7 %collective-permute-start.22 = (bf16[8,3072]{1,0:T(8,128)(2,1)S(1)}, bf16[8,3072]{1,0:T(8,128)(2,1)S(1)}, u32[]{:S(2)}, u32[]{:S(2)}) collective-permute-start(bf16[8,3072]{1,0:T(8,128)(2,1)S(1)} %get-tuple-element.28), channel_id=1, source_target_pairs={{0,4},{4,0},{8,12},{12,8},{1,5},{5,1},{9,13},{13,9},{2,6},{6,2},{1... | collective-permute-start | bytes 147464 | tf_op jit(solution)/shard_map/ppermute | solution.py:284
  108.3 5.1 %collective-permute-start.21 = (bf16[8,3072]{1,0:T(8,128)(2,1)S(1)}, bf16[8,3072]{1,0:T(8,128)(2,1)S(1)}, u32[]{:S(2)}, u32[]{:S(2)}) collective-permute-start(bf16[8,3072]{1,0:T(8,128)(2,1)S(1)} %get-tuple-element.29), channel_id=1, source_target_pairs={{0,8},{4,12},{8,0},{12,4},{1,9},{5,13},{9,1},{13,5},{2,10},{6,14},... | collective-permute-start | bytes 147464 | tf_op jit(solution)/shard_map/ppermute | solution.py:284
